TPU v7x, 32 devices: a whole 2x2x4 slice. The times are simulated.
32 devices in a mesh: dp: 8 (over y, x, core), tensor: 4 (over z).
Axes of the slice: x: 2, y: 2, z: 4, core: 2. Of those that a mesh axis runs over, the one named last changes fastest.
Arguments:
- inputs: bfloat16 [2048, 2048], P(('dp', 'tensor')), parts along dimension 0, may hold values from -6 to 6
- grad_out: bfloat16 [2048, 2048], P(('dp', 'tensor')), parts along dimension 0, may hold values from -6 to 6
- gate_weight: bfloat16 [2048, 7168], P(None, 'tensor'), may hold values from -6 to 6
- up_weight: bfloat16 [2048, 7168], P(None, 'tensor'), may hold values from -6 to 6
- down_weight: bfloat16 [7168, 2048], P('tensor'), may hold values from -6 to 6
Outputs:
- grad_inputs: bfloat16 [2048, 2048], P(('dp', 'tensor')), parts along dimension 0
- grad_gate: bfloat16 [16384, 7168], P('dp', 'tensor'), parts along dimension 0
- grad_up: bfloat16 [16384, 7168], P('dp', 'tensor'), parts along dimension 0
- grad_down: bfloat16 [57344, 2048], P(('dp', 'tensor')), parts along dimension 0
There are 8 independent parts, one for each index of `dp`. A program takes and returns all parts, laid end to end along the dimension named above; an argument that names none is the same for every part. Nothing has to cross between parts.
All inputs are finite; a program needn't handle non-finite values.
Results may differ from a plain program's by a relative error of at most 0.0049.
Values may be sent and summed in bfloat16 or wider, within the bound.
A program may use at most 128 MiB of HBM per device.

v0:
```python
import jax
import jax.numpy as jnp
from jax import lax
from jax.sharding import PartitionSpec as P

D = 2048
FF = 7168


def contract_last(left, right):
    return lax.dot_general(
        left, right, (((1,), (1,)), ((), ())), preferred_element_type=jnp.float32
    )


def contract_first(left, right):
    return lax.dot_general(
        left, right, (((0,), (0,)), ((), ())), preferred_element_type=jnp.float32
    )


def on_device(inputs, grad_out, gate_weight, up_weight, down_weight):
    tokens_all = lax.all_gather(inputs, "tensor", axis=0, tiled=True)
    grads_all = lax.all_gather(grad_out, "tensor", axis=0, tiled=True)
    inv_width = D ** (-0.5)
    inv_rows = tokens_all.shape[0] ** (-0.5)
    inv_hidden = (2 * FF) ** (-0.5)
    gate = jnp.dot(tokens_all, gate_weight, preferred_element_type=jnp.float32) * inv_width
    up = jnp.dot(tokens_all, up_weight, preferred_element_type=jnp.float32) * inv_width
    sig = jax.nn.sigmoid(gate)
    act = gate * sig
    hidden = (act * up).astype(jnp.bfloat16)
    d_hidden = contract_last(grads_all, down_weight) * inv_width
    grad_down = (contract_first(hidden, grads_all) * inv_rows).astype(jnp.bfloat16)
    d_gate = (d_hidden * up * sig * (1.0 + gate * (1.0 - sig))).astype(jnp.bfloat16)
    d_up = (d_hidden * act).astype(jnp.bfloat16)
    grad_gate = (contract_first(tokens_all, d_gate) * inv_rows).astype(jnp.bfloat16)
    grad_up = (contract_first(tokens_all, d_up) * inv_rows).astype(jnp.bfloat16)
    summed = lax.psum_scatter(
        contract_last(d_gate, gate_weight) * inv_hidden
        + contract_last(d_up, up_weight) * inv_hidden,
        "tensor",
        scatter_dimension=0,
        tiled=True,
    )
    grad_inputs = summed.astype(jnp.bfloat16)
    return (grad_inputs, grad_gate, grad_up, grad_down)


def solution(mesh):
    placed = (
        P(("dp", "tensor"), None),
        P(("dp", "tensor"), None),
        P(None, "tensor"),
        P(None, "tensor"),
        P("tensor", None),
    )
    return jax.shard_map(
        on_device,
        mesh=mesh,
        in_specs=placed,
        out_specs=(
            P(("dp", "tensor"), None),
            P("dp", "tensor"),
            P("dp", "tensor"),
            P(("dp", "tensor"), None),
        ),
        check_vma=False,
    )
```

profile of v0, /device:TPU:0, one launch (start us, length us, event | category | flops | bytes accessed | tf_op | source)
XLA Modules:
  0.0 139.9 jit_solution(8619819542554499196)
XLA Ops:
  7.2 0.0 all-gather.5.cloned.1.call-start
  7.2 0.7 all-gather.5.cloned.1.call-update
  7.9 0.0 all-gather.3.cloned.1.call-start
  7.9 0.7 all-gather.3.cloned.1.call-update
  8.6 0.0 reduce-scatter.2.cloned.1.call-start
  8.7 31.5 %all-gather.5.cloned.1.call-done = bf16[256,2048]{1,0:T(8,128)(2,1)} async-done(((bf16[64,2048]{1,0:T(8,128)(2,1)}), bf16[256,2048]{1,0:T(8,128)(2,1)}) %all-gather.5.cloned.1.call-update) | async-done | bytes 1048592 | tf_op jit(solution)/shard_map/all_gather | solution.py:23
  40.2 0.0 copy-start
  40.2 6.8 %convolution_multiply_fusion = f32[256,1792]{1,0:T(8,128)} fusion(bf16[256,2048]{1,0:T(8,128)(2,1)} %all-gather.5.cloned.1.call-done, bf16[2048,1792]{1,0:T(8,128)(2,1)} %param.7), kind=kOutput, calls=%fused_computation.5 | convolution fusion | flops 1879506944 | bytes 10223616 | tf_op jit(solution)/shard_map/dot_general | solution.py:28
  47.0 0.0 copy-done
  47.0 6.6 %convolution_multiply_fusion.1 = f32[256,1792]{1,0:T(8,128)} fusion(bf16[256,2048]{1,0:T(8,128)(2,1)S(1)} %copy-done, bf16[2048,1792]{1,0:T(8,128)(2,1)} %param.8), kind=kOutput, calls=%fused_computation.6 | convolution fusion | flops 1879506944 | bytes 10223616 | tf_op jit(solution)/shard_map/dot_general | solution.py:29
  53.6 15.6 %all-gather.3.cloned.1.call-done = bf16[256,2048]{1,0:T(8,128)(2,1)} async-done(((bf16[64,2048]{1,0:T(8,128)(2,1)}), bf16[256,2048]{1,0:T(8,128)(2,1)}) %all-gather.3.cloned.1.call-update) | async-done | bytes 1048592 | tf_op jit(solution)/shard_map/all_gather | solution.py:24
  69.3 7.1 %multiply_convert_fusion.4 = (bf16[256,1792]{1,0:T(8,128)(2,1)S(1)}, bf16[256,1792]{1,0:T(8,128)(2,1)S(1)}) fusion(f32[256,1792]{1,0:T(8,128)} %convolution_multiply_fusion, f32[256,1792]{1,0:T(8,128)} %convolution_multiply_fusion.1, bf16[256,2048]{1,0:T(8,128)(2,1)} %all-gather.3.cloned.1.call-done, bf16[1792,2048]{1,0:T(8,128)(2,1)} %param.9), kind=kOutput, calls=%fused_computation.11 | convolution fusion | flops 1885470720 | bytes 13893632 | tf_op jit(solution)/shard_map/dot_general | solution.py:11
  76.3 5.2 %fusion.6 = f32[256,2048]{1,0:T(8,128)S(1)} fusion(bf16[256,1792]{1,0:T(8,128)(2,1)S(1)} %get-tuple-element.9, bf16[2048,1792]{1,0:T(8,128)(2,1)} %param.7), kind=kOutput, calls=%fused_computation.16 | convolution fusion | flops 1879048192 | bytes 10354688 | tf_op jit(solution)/shard_map/dot_general | solution.py:11
  81.5 6.6 %fusion.2 = f32[256,2048]{1,0:T(8,128)} fusion(f32[256,2048]{1,0:T(8,128)S(1)} %fusion.6, bf16[256,1792]{1,0:T(8,128)(2,1)S(1)} %get-tuple-element.8, bf16[2048,1792]{1,0:T(8,128)(2,1)} %param.8), kind=kOutput, calls=%fused_computation.9 | convolution fusion | flops 1880096768 | bytes 12451840 | tf_op jit(solution)/shard_map/dot_general | solution.py:11
  88.1 0.0 reduce-scatter.2.cloned.1.call-update
  88.1 5.2 %fusion.1 = bf16[2048,1792]{0,1:T(8,128)(2,1)} fusion(bf16[256,1792]{1,0:T(8,128)(2,1)S(1)} %get-tuple-element.8, bf16[256,2048]{1,0:T(8,128)(2,1)S(1)} %copy-done), kind=kOutput, calls=%fused_computation.4 | convolution fusion | flops 1886388224 | bytes 9306112 | tf_op jit(solution)/shard_map/dot_general | solution.py:17
  93.2 10.1 %copy.10 = bf16[2048,1792]{1,0:T(8,128)(2,1)} copy(bf16[2048,1792]{0,1:T(8,128)(2,1)} %fusion.1) | data formatting | bytes 14680064
  103.3 5.1 %fusion = bf16[2048,1792]{0,1:T(8,128)(2,1)} fusion(bf16[256,1792]{1,0:T(8,128)(2,1)S(1)} %get-tuple-element.9, bf16[256,2048]{1,0:T(8,128)(2,1)S(1)} %copy-done), kind=kOutput, calls=%fused_computation.3 | convolution fusion | flops 1886388224 | bytes 9306112 | tf_op jit(solution)/shard_map/dot_general | solution.py:17
  108.5 0.0 copy-start.1
  108.5 0.0 copy-start.2
  108.5 10.1 %copy.9 = bf16[2048,1792]{1,0:T(8,128)(2,1)} copy(bf16[2048,1792]{0,1:T(8,128)(2,1)} %fusion) | data formatting | bytes 14680064
  118.6 0.0 copy-done.1
  118.6 0.0 copy-done.2
  118.6 6.8 %multiply_convert_fusion = bf16[1792,2048]{1,0:T(8,128)(2,1)} fusion(bf16[256,2048]{1,0:T(8,128)(2,1)S(1)} %copy-done.1, f32[256,1792]{1,0:T(8,128)} %convolution_multiply_fusion.1, f32[256,1792]{1,0:T(8,128)S(1)} %copy-done.2), kind=kOutput, calls=%fused_computation | convolution fusion | flops 1889140736 | bytes 12058624 | tf_op jit(solution)/shard_map/dot_general | solution.py:17
  125.4 6.2 %reduce-scatter.2.cloned.1.call-done = f32[64,2048]{1,0:T(8,128)} async-done(((f32[256,2048]{1,0:T(8,128)}), f32[64,2048]{1,0:T(8,128)}) %reduce-scatter.2.cloned.1.call-update) | async-done | bytes 524304 | tf_op jit(solution)/shard_map/reduce_scatter | solution.py:39
  131.6 1.8 %convert_element_type.29 = bf16[64,2048]{1,0:T(8,128)(2,1)} convert(f32[64,2048]{1,0:T(8,128)} %reduce-scatter.2.cloned.1.call-done) | non-fusion elementwise | flops 131072 | bytes 786432 | tf_op jit(solution)/shard_map/convert_element_type | solution.py:46
Async XLA Ops:
  7.2 33.1 %all-gather.5.cloned.1.call-start = ((), (), s32[]{:S(2)}) async-start(), calls=%async_computation.2 | async-start | bytes 1310720 | tf_op jit(solution)/shard_map/all_gather | solution.py:23
  7.9 61.4 %all-gather.3.cloned.1.call-start = ((), (), s32[]{:S(2)}) async-start(), calls=%async_computation.1 | async-start | bytes 1310720 | tf_op jit(solution)/shard_map/all_gather | solution.py:24
  8.6 122.9 %reduce-scatter.2.cloned.1.call-start = ((), (), s32[]{:S(2)}) async-start(), calls=%async_computation.3 | async-start | bytes 2621440 | tf_op jit(solution)/shard_map/reduce_scatter | solution.py:39
  40.2 6.8 %copy-start = (bf16[256,2048]{1,0:T(8,128)(2,1)S(1)}, bf16[256,2048]{1,0:T(8,128)(2,1)}, u32[]{:S(2)}) copy-start(bf16[256,2048]{1,0:T(8,128)(2,1)} %all-gather.5.cloned.1.call-done) | copy-start | bytes 3145732
  108.5 10.1 %copy-start.1 = (bf16[256,2048]{1,0:T(8,128)(2,1)S(1)}, bf16[256,2048]{1,0:T(8,128)(2,1)}, u32[]{:S(2)}) copy-start(bf16[256,2048]{1,0:T(8,128)(2,1)} %all-gather.3.cloned.1.call-done) | copy-start | bytes 3145732
  108.5 10.1 %copy-start.2 = (f32[256,1792]{1,0:T(8,128)S(1)}, f32[256,1792]{1,0:T(8,128)}, u32[]{:S(2)}) copy-start(f32[256,1792]{1,0:T(8,128)} %convolution_multiply_fusion) | copy-start | bytes 5505028
Sparse Core Ops, SparseCore 0:
  9.6 30.6 all-gather.4
  41.8 27.4 all-gather.2
  88.2 43.3 reduce-scatter.1
where the time goes:
time: 141 us; the launch traced here: 140 us
  waiting for transfers between devices  54.7 us (39%)
  matrix products  49.3 us (35%)
  local copies, waits for them, and re-layouts  20.2 us (14%)
  between operations  13.8 us (10%)
  other arithmetic  1.77 us (1%)
    all_gather x1, waiting for transfers between devices, on_device(): tokens_all = lax.all_gather(inputs, 'tensor', axis=0, tiled=True)  31.5 us
    unnamed x8, local copies, waits for them, and re-layouts  20.2 us
    dot_general x3, matrix products, contract_last(): lax.dot_general(left, right, (((1,), (1,)), ((), ())), preferred_element_...  18.8 us
    dot_general x3, matrix products, contract_first(): lax.dot_general(left, right, (((0,), (0,)), ((), ())), preferred_element_...  17.1 us
    all_gather x1, waiting for transfers between devices, on_device(): grads_all = lax.all_gather(grad_out, 'tensor', axis=0, tiled=True)  15.6 us
    dot_general x1, matrix products, on_device(): jnp.dot(tokens_all, gate_weight, preferred_element_type=jnp.float32)  6.77 us
    dot_general x1, matrix products, on_device(): jnp.dot(tokens_all, up_weight, preferred_element_type=jnp.float32)  6.64 us
    reduce_scatter x1, waiting for transfers between devices, on_device(): lax.psum_scatter(contract_last(d_gate, gate_weight) * inv_hidden + contra...  6.19 us
  transfers between devices with their start and end apart: 3, of which 3 were waited for; matrix products, arithmetic and copies ran while one was open for 36% of the time, Pallas kernels for 0%

commit v1 on v0

--- a/solution.py
+++ b/solution.py
@@ -2,9 +2,16 @@
 import jax.numpy as jnp
 from jax import lax
 from jax.sharding import PartitionSpec as P
+from jax.lax import all_gather
 
 D = 2048
 FF = 7168
+
+
+def lane_mix(point, slab_in, chip_axis):
+    formed = jnp.concatenate([point, slab_in], axis=1)
+    part_next = all_gather(formed, chip_axis, axis=0, tiled=True)
+    return jnp.split(part_next, [point.shape[1]], axis=1)
 
 
 def contract_last(left, right):
@@ -20,8 +27,7 @@
 
 
 def on_device(inputs, grad_out, gate_weight, up_weight, down_weight):
-    tokens_all = lax.all_gather(inputs, "tensor", axis=0, tiled=True)
-    grads_all = lax.all_gather(grad_out, "tensor", axis=0, tiled=True)
+    tokens_all, grads_all = lane_mix(inputs, grad_out, "tensor")
     inv_width = D ** (-0.5)
     inv_rows = tokens_all.shape[0] ** (-0.5)
     inv_hidden = (2 * FF) ** (-0.5)

time: 141 us -> 136 us (0.965)
  waiting for transfers between devices: 54.7 us -> 76.5 us
  local copies, waits for them, and re-layouts: 20.2 us -> 0.04 us
  matrix products: 49.3 us -> 41.7 us
  other arithmetic: 1.77 us -> 3.63 us
    reduce_scatter x1, waiting for transfers between devices: 6.19 us -> 26.8 us  [on_device(): lax.psum_scatter(contract_last(d_gate, gate_weight) * inv_hidden + contra...]
    unnamed x8 -> x20, local copies, waits for them, and re-layouts: 20.2 us -> 0.04 us
    dot_general x3, matrix products: 18.8 us -> 12.5 us  [contract_last(): lax.dot_general(left, right, (((1,), (1,)), ((), ())), preferred_element_...]
    all_gather x2 -> x1, waiting for transfers between devices: 47.1 us -> 49.7 us  [lane_mix(): part_next = all_gather(formed, chip_axis, axis=0, tiled=True)]
    concatenate x0 -> x1, other arithmetic: none -> 1.86 us  [lane_mix(): formed = jnp.concatenate([point, slab_in], axis=1)]
  transfers between devices with their start and end apart: 3 -> 2, of which waited for: 3 -> 2; matrix products, arithmetic and copies ran while one was open for 36% -> 12% of each run, Pallas kernels for 0% -> 0%
where the time goes in v1:
time: 136 us
  waiting for transfers between devices  76.5 us (56%)
  matrix products  41.7 us (31%)
  between operations  14.1 us (10%)
  other arithmetic  3.63 us (3%)
    all_gather x1, waiting for transfers between devices, lane_mix(): part_next = all_gather(formed, chip_axis, axis=0, tiled=True)  49.7 us
    reduce_scatter x1, waiting for transfers between devices, on_device(): lax.psum_scatter(contract_last(d_gate, gate_weight) * inv_hidden + contra...  26.8 us
    dot_general x3, matrix products, contract_first(): lax.dot_general(left, right, (((0,), (0,)), ((), ())), preferred_element_...  15.9 us
    dot_general x3, matrix products, contract_last(): lax.dot_general(left, right, (((1,), (1,)), ((), ())), preferred_element_...  12.5 us
    dot_general x1, matrix products, on_device(): jnp.dot(tokens_all, gate_weight, preferred_element_type=jnp.float32)  6.84 us
    dot_general x1, matrix products, on_device(): jnp.dot(tokens_all, up_weight, preferred_element_type=jnp.float32)  6.51 us
  transfers between devices with their start and end apart: 2, of which 2 were waited for; matrix products, arithmetic and copies ran while one was open for 12% of the time, Pallas kernels for 0%

profile of v1, /device:TPU:0, one launch (start us, length us, event | category | flops | bytes accessed | tf_op | source)
XLA Modules:
  0.0 136.1 jit_solution(15537065447585243660)
XLA Ops:
  7.2 0.0 all-gather.2.cloned.1.call-start
  7.2 1.9 %pad_maximum_fusion = bf16[64,4096]{1,0:T(8,128)(2,1)} fusion(bf16[64,2048]{1,0:T(8,128)(2,1)} %param.6, bf16[64,2048]{1,0:T(8,128)(2,1)} %param.5), kind=kLoop, calls=%fused_computation.19 | loop fusion | flops 1048576 | bytes 1048576 | tf_op jit(solution)/shard_map/concatenate | solution.py:12
  9.1 0.0 all-gather.2.cloned.1.call-update
  9.1 0.0 reduce-scatter.2.cloned.1.call-start
  9.1 49.7 %all-gather.2.cloned.1.call-done = bf16[256,4096]{1,0:T(8,128)(2,1)} async-done(((bf16[64,4096]{1,0:T(8,128)(2,1)}), bf16[256,4096]{1,0:T(8,128)(2,1)}) %all-gather.2.cloned.1.call-update) | async-done | bytes 2097168 | tf_op jit(solution)/shard_map/all_gather | solution.py:13
  58.8 0.0 slice-start
  58.8 6.8 %convolution_multiply_fusion = f32[256,1792]{1,0:T(8,128)} fusion(bf16[2048,1792]{1,0:T(8,128)(2,1)} %param.7, bf16[256,4096]{1,0:T(8,128)(2,1)} %all-gather.2.cloned.1.call-done), kind=kOutput, calls=%fused_computation.3 | convolution fusion | flops 1879506944 | bytes 10223616 | tf_op jit(solution)/shard_map/dot_general | solution.py:34
  65.7 0.0 copy-done
  65.7 0.0 slice-start.1
  65.7 0.0 slice-start.2
  65.7 0.0 slice-start.4
  65.7 6.5 %convolution_multiply_fusion.1 = f32[256,1792]{1,0:T(8,128)} fusion(bf16[2048,1792]{1,0:T(8,128)(2,1)} %param.8, bf16[256,4096]{1,0:T(8,128)(2,1)S(1)} %copy-done), kind=kOutput, calls=%fused_computation.4 | convolution fusion | flops 1879506944 | bytes 10223616 | tf_op jit(solution)/shard_map/dot_general | solution.py:35
  72.2 0.0 slice-done
  72.2 0.0 slice-done.1
  72.2 0.0 slice-start.5
  72.2 5.8 %multiply_convert_fusion.4 = (bf16[256,1792]{1,0:T(8,128)(2,1)S(1)}, bf16[256,1792]{1,0:T(8,128)(2,1)}) fusion(f32[256,1792]{1,0:T(8,128)} %convolution_multiply_fusion, f32[256,1792]{1,0:T(8,128)} %convolution_multiply_fusion.1, bf16[1792,2048]{1,0:T(8,128)(2,1)S(1)} %bitcast.10, bf16[256,4096]{1,0:T(8,128)(2,1)S(1)} %copy-done), kind=kOutput, calls=%fused_computation.9 | convolution fusion | flops 1885470720 | bytes 13893632 | tf_op jit(solution)/shard_map/dot_general | solution.py:18
  78.0 0.0 slice-done.2
  78.0 0.0 slice-done.3
  78.0 3.3 %fusion.10 = f32[256,2048]{1,0:T(8,128)S(1)} fusion(bf16[256,1792]{1,0:T(8,128)(2,1)} %get-tuple-element.5, bf16[2048,1792]{1,0:T(8,128)(2,1)S(1)} %bitcast.12), kind=kOutput, calls=%fused_computation.21 | convolution fusion | flops 1879048192 | bytes 10354688 | tf_op jit(solution)/shard_map/dot_general | solution.py:18
  81.2 0.0 slice-done.4
  81.3 0.0 slice-done.5
  81.3 3.5 %fusion = f32[256,2048]{1,0:T(8,128)} fusion(f32[256,2048]{1,0:T(8,128)S(1)} %fusion.10, bf16[256,1792]{1,0:T(8,128)(2,1)S(1)} %get-tuple-element.4, bf16[2048,1792]{1,0:T(8,128)(2,1)S(1)} %bitcast.14), kind=kOutput, calls=%fused_computation.7 | convolution fusion | flops 1880096768 | bytes 12451840 | tf_op jit(solution)/shard_map/dot_general | solution.py:18
  84.7 0.0 reduce-scatter.2.cloned.1.call-update
  84.8 0.0 copy-start.1
  84.8 5.2 %multiply_convert_fusion.1 = bf16[2048,1792]{1,0:T(8,128)(2,1)} fusion(bf16[256,1792]{1,0:T(8,128)(2,1)S(1)} %get-tuple-element.4, bf16[256,4096]{1,0:T(8,128)(2,1)S(1)} %copy-done), kind=kOutput, calls=%fused_computation.1 | convolution fusion | flops 1886388224 | bytes 9306112 | tf_op jit(solution)/shard_map/dot_general | solution.py:24
  90.0 0.0 copy-done.1
  90.0 5.4 %multiply_convert_fusion.2 = bf16[2048,1792]{1,0:T(8,128)(2,1)} fusion(bf16[256,1792]{1,0:T(8,128)(2,1)S(1)} %copy-done.1, bf16[256,4096]{1,0:T(8,128)(2,1)S(1)} %copy-done), kind=kOutput, calls=%fused_computation.2 | convolution fusion | flops 1886388224 | bytes 9306112 | tf_op jit(solution)/shard_map/dot_general | solution.py:24
  95.4 0.0 copy-done.2
  95.4 0.0 copy-done.3
  95.4 5.3 %multiply_convert_fusion = bf16[1792,2048]{1,0:T(8,128)(2,1)} fusion(bf16[256,4096]{1,0:T(8,128)(2,1)S(1)} %copy-done, f32[256,1792]{1,0:T(8,128)S(1)} %copy-done.3, f32[256,1792]{1,0:T(8,128)S(1)} %copy-done.2), kind=kOutput, calls=%fused_computation | convolution fusion | flops 1889140736 | bytes 12058624 | tf_op jit(solution)/shard_map/dot_general | solution.py:24
  100.7 26.8 %reduce-scatter.2.cloned.1.call-done = f32[64,2048]{1,0:T(8,128)} async-done(((f32[256,2048]{1,0:T(8,128)}), f32[64,2048]{1,0:T(8,128)}) %reduce-scatter.2.cloned.1.call-update) | async-done | bytes 524304 | tf_op jit(solution)/shard_map/reduce_scatter | solution.py:45
  127.5 1.8 %convert_element_type.23 = bf16[64,2048]{1,0:T(8,128)(2,1)} convert(f32[64,2048]{1,0:T(8,128)} %reduce-scatter.2.cloned.1.call-done) | non-fusion elementwise | flops 131072 | bytes 786432 | tf_op jit(solution)/shard_map/convert_element_type | solution.py:52
  (7 shorter events, 0.0 us)
Async XLA Ops:
  7.2 51.6 %all-gather.2.cloned.1.call-start = ((), (), s32[]{:S(2)}) async-start(), calls=%async_computation.1 | async-start | bytes 2621440 | tf_op jit(solution)/shard_map/all_gather | solution.py:13
  9.1 118.4 %reduce-scatter.2.cloned.1.call-start = ((), (), s32[]{:S(2)}) async-start(), calls=%async_computation.2 | async-start | bytes 2621440 | tf_op jit(solution)/shard_map/reduce_scatter | solution.py:45
  58.8 6.8 %copy-start = (bf16[256,4096]{1,0:T(8,128)(2,1)S(1)}, bf16[256,4096]{1,0:T(8,128)(2,1)}, u32[]{:S(2)}) copy-start(bf16[256,4096]{1,0:T(8,128)(2,1)} %all-gather.2.cloned.1.call-done) | copy-start | bytes 6291460
  58.8 13.4 %slice-start = ((s8[7340032]{0:T(1024)(128)(4,1)}), s8[4194304]{0:T(1024)(128)(4,1)S(1)}, s32[]{:S(2)}) async-start(s8[7340032]{0:T(1024)(128)(4,1)} %bitcast.9), calls=%async_computation.3 | async-start | bytes 8388608
  65.7 6.5 %slice-start.1 = ((s8[7340032]{0:T(1024)(128)(4,1)}), s8[3145728]{0:T(1024)(128)(4,1)S(1)}, s32[]{:S(2)}) async-start(s8[7340032]{0:T(1024)(128)(4,1)} %bitcast.9), calls=%async_computation.4 | async-start | bytes 6291456
  65.7 12.3 %slice-start.2 = ((s8[7340032]{0:T(1024)(128)(4,1)}), s8[4194304]{0:T(1024)(128)(4,1)S(1)}, s32[]{:S(2)}) async-start(s8[7340032]{0:T(1024)(128)(4,1)} %bitcast.11), calls=%async_computation.5 | async-start | bytes 8388608
  65.7 15.6 %slice-start.4 = ((s8[7340032]{0:T(1024)(128)(4,1)}), s8[4194304]{0:T(1024)(128)(4,1)S(1)}, s32[]{:S(2)}) async-start(s8[7340032]{0:T(1024)(128)(4,1)} %bitcast.13), calls=%async_computation.7 | async-start | bytes 8388608
  72.2 5.8 %slice-start.3 = ((s8[7340032]{0:T(1024)(128)(4,1)}), s8[3145728]{0:T(1024)(128)(4,1)S(1)}, s32[]{:S(2)}) async-start(s8[7340032]{0:T(1024)(128)(4,1)} %bitcast.11), calls=%async_computation.6 | async-start | bytes 6291456
  72.2 9.1 %slice-start.5 = ((s8[7340032]{0:T(1024)(128)(4,1)}), s8[3145728]{0:T(1024)(128)(4,1)S(1)}, s32[]{:S(2)}) async-start(s8[7340032]{0:T(1024)(128)(4,1)} %bitcast.13), calls=%async_computation.8 | async-start | bytes 6291456
  84.8 5.2 %copy-start.1 = (bf16[256,1792]{1,0:T(8,128)(2,1)S(1)}, bf16[256,1792]{1,0:T(8,128)(2,1)}, u32[]{:S(2)}) copy-start(bf16[256,1792]{1,0:T(8,128)(2,1)} %get-tuple-element.5) | copy-start | bytes 2752516
  90.0 5.4 %copy-start.2 = (f32[256,1792]{1,0:T(8,128)S(1)}, f32[256,1792]{1,0:T(8,128)}, u32[]{:S(2)}) copy-start(f32[256,1792]{1,0:T(8,128)} %convolution_multiply_fusion) | copy-start | bytes 5505028
  90.0 5.4 %copy-start.3 = (f32[256,1792]{1,0:T(8,128)S(1)}, f32[256,1792]{1,0:T(8,128)}, u32[]{:S(2)}) copy-start(f32[256,1792]{1,0:T(8,128)} %convolution_multiply_fusion.1) | copy-start | bytes 5505028
Sparse Core Ops, SparseCore 0:
  10.1 48.6 all-gather.1
  84.9 42.5 reduce-scatter.1
